TPU v7x, 32 devices: a whole 2x2x4 slice. The times are simulated.
32 devices in a mesh: dp: 8 (over z, x), tensor: 4 (over y, core).
Axes of the slice: x: 2, y: 2, z: 4, core: 2. Of those that a mesh axis runs over, the one named last changes fastest.
Arguments:
- context: bfloat16 [2, 8192, 3072], P(None, 'dp', 'tensor'), may hold values from -6 to 6
- out_grad: bfloat16 [2, 8192, 3072], P(None, ('dp', 'tensor')), may hold values from -0.1875 to 0.1875
- error_in: bfloat16 [2, 24576, 3072], P(None, 'dp', 'tensor'), may hold values from -6 to 6
- right_init: float32 [2, 64, 3072], P(None, None, 'tensor'), may hold values from -6 to 6
Outputs:
- summed_update: bfloat16 [2, 3072, 3072], P(None, 'dp', 'tensor')
- error_out: bfloat16 [2, 24576, 3072], P(None, 'dp', 'tensor')
All inputs are finite; a program needn't handle non-finite values.
Results may differ from a plain program's by a relative error of at most 0.015.
Values may be sent and summed in bfloat16 or wider, within the bound.
A program may use at most 128 MiB of HBM per device.

v0:
```python
import jax
import jax.numpy as jnp
from jax import lax
from jax.sharding import PartitionSpec as P


def solve_rows(gram_matrix, left_factor):
    ridge_term = 1e-06 * jnp.mean(jnp.diagonal(gram_matrix, axis1=1, axis2=2), axis=1)
    eye_matrix = jnp.eye(gram_matrix.shape[1], dtype=gram_matrix.dtype)
    gram_matrix = gram_matrix + ridge_term[:, None, None] * eye_matrix
    factor_low = jnp.linalg.cholesky(gram_matrix)

    def one_solve(low_part, rhs_part):
        return jax.scipy.linalg.solve_triangular(low_part, rhs_part, lower=True)

    return jax.vmap(one_solve)(factor_low, left_factor)


def gram_of(left_factor):
    return jnp.einsum("lrd,lsd->lrs", left_factor, left_factor, precision=lax.Precision.HIGHEST)


def compress(context, out_grad, error_in, right_init):
    out_width = out_grad.shape[2]
    moment = jnp.einsum(
        "ltd,lte->lde",
        lax.all_gather(out_grad, "tensor", axis=1, tiled=True),
        context,
        preferred_element_type=jnp.float32,
    )
    moment = moment + error_in.astype(jnp.float32)
    left_factor = jnp.einsum("lre,lde->lrd", right_init, moment, precision=lax.Precision.HIGHEST)
    left_part = lax.psum_scatter(left_factor, "tensor", scatter_dimension=2, tiled=True)
    left_part = lax.psum(left_part, "dp")
    gram_matrix = lax.psum(gram_of(left_part), "tensor")
    ortho_part = solve_rows(gram_matrix, left_part)
    ortho_basis = lax.all_gather(ortho_part, "tensor", axis=2, tiled=True)
    right_terms = jnp.einsum("lrd,lde->lre", ortho_basis, moment, precision=lax.Precision.HIGHEST)
    right_factor = lax.psum(right_terms.astype(jnp.bfloat16), "dp").astype(jnp.float32)
    replicas = lax.axis_size("dp")
    row_share = out_width // replicas
    own_basis = lax.dynamic_slice_in_dim(
        ortho_basis, lax.axis_index("dp") * row_share, row_share, 2
    )
    summed = jnp.einsum("lrd,lre->lde", own_basis, right_factor, precision=lax.Precision.HIGHEST)
    mean_part = jnp.einsum(
        "lrd,lre->lde", ortho_basis, right_factor / replicas, precision=lax.Precision.HIGHEST
    )
    new_error = (moment - mean_part).astype(jnp.bfloat16)
    return (summed.astype(jnp.bfloat16), new_error)


def body(context, out_grad, error_in, right_init):
    return compress(context, out_grad, error_in, right_init)


def solution(mesh):
    return jax.shard_map(
        body,
        mesh=mesh,
        in_specs=(
            P(None, "dp", "tensor"),
            P(None, ("dp", "tensor"), None),
            P(None, "dp", "tensor"),
            P(None, None, "tensor"),
        ),
        out_specs=(P(None, "dp", "tensor"), P(None, "dp", "tensor")),
        check_vma=False,
    )
```

profile of v0, /device:TPU:0, one launch (start us, length us, event | category | flops | bytes accessed | tf_op | source)
XLA Modules:
  0.0 419.1 jit_solution(9212171889300298580)
XLA Ops:
  7.2 0.0 all-gather.3.cloned.1.call-start
  7.2 4.8 %copy.12 = bf16[2,256,3072]{1,2,0:T(8,128)(2,1)} copy(bf16[2,256,3072]{2,1,0:T(8,128)(2,1)} %param.5) | data formatting | bytes 6291456 | tf_op args[1]
  12.0 0.0 all-gather.3.cloned.1.call-update
  12.0 0.0 reduce-scatter.2.cloned.1.call-start
  12.1 86.6 %all-gather.3.cloned.1.call-done = bf16[2,1024,3072]{1,2,0:T(8,128)(2,1)} async-done(((bf16[2,256,3072]{1,2,0:T(8,128)(2,1)}), bf16[2,1024,3072]{1,2,0:T(8,128)(2,1)}) %all-gather.3.cloned.1.call-update) | async-done | bytes 12582928 | tf_op jit(solution)/shard_map/all_gather | solution.py:27
  98.7 19.3 %convert_add_fusion = f32[2,3072,768]{2,1,0:T(8,128)} fusion(bf16[2,3072,768]{2,1,0:T(8,128)(2,1)} %param.6, bf16[2,1024,3072]{1,2,0:T(8,128)(2,1)} %all-gather.3.cloned.1.call-done, bf16[2,1024,768]{2,1,0:T(8,128)(2,1)S(1)} %copy-done), kind=kOutput, calls=%fused_computation.2 | convolution fusion | flops 9673113600 | bytes 44040192 | tf_op jit(solution)/shard_map/ltd,lte->lde/dot_general | solution.py:25
  118.0 22.5 %convolution_bitcast_fusion = f32[2,64,3072]{2,1,0:T(8,128)} fusion(f32[2,3072,768]{2,1,0:T(8,128)} %convert_add_fusion, f32[2,64,768]{2,1,0:T(8,128)S(1)} %copy-done.4), kind=kOutput, calls=%fused_computation.3 | convolution fusion | flops 3623878656 | bytes 20840448 | tf_op jit(solution)/shard_map/lre,lde->lrd/dot_general | solution.py:32
  140.5 0.0 all-reduce.3.cloned.1.call-start
  140.5 28.1 %reduce-scatter.2.cloned.1.call-done = f32[2,64,768]{2,1,0:T(8,128)} async-done(((f32[2,64,3072]{2,1,0:T(8,128)}), f32[2,64,768]{2,1,0:T(8,128)}) %reduce-scatter.2.cloned.1.call-update) | async-done | bytes 393232 | tf_op jit(solution)/shard_map/reduce_scatter | solution.py:33
  168.6 0.0 all-reduce.3.cloned.1.call-update
  168.7 0.0 all-gather.5.cloned.1.call-start
  168.7 0.1 copy.15
  168.9 75.0 %all-reduce.3.cloned.1.call-done = f32[2,64,768]{2,1,0:T(8,128)} async-done(((f32[2,64,768]{2,1,0:T(8,128)}), f32[2,64,768]{2,1,0:T(8,128)}) %all-reduce.3.cloned.1.call-update) | async-done | bytes 393232 | tf_op jit(solution)/shard_map/psum | solution.py:34
  243.9 1.7 fusion.10
  245.5 10.9 %psum.22 = f32[2,64,64]{1,2,0:T(8,128)S(1)} all-reduce(f32[2,64,64]{1,2,0:T(8,128)S(1)} %fusion.10), channel_id=1, replica_groups=mesh['dp'=8,'tensor'=4] {'tensor'}, use_global_device_ids=true, to_apply=%region_2.0 | all-reduce | flops 8192 | bytes 65536 | tf_op jit(solution)/shard_map/psum | solution.py:35
  256.4 1.9 copy.14
  258.3 0.9 gather_fusion
  259.3 0.1 multiply_add_fusion
  259.3 0.1 copy.16
  259.4 0.1 fusion.6
  259.5 11.7 %custom-call.8 = f32[2,64,64]{2,1,0:T(8,128)S(1)} custom-call(f32[2,64,64]{2,1,0:T(8,128)S(1)} %fusion.6), custom_call_target="Cholesky" | custom-call | tf_op jit(solution)/shard_map/jit(cholesky)/cholesky | solution.py:11
  271.3 0.1 compare_reduce_fusion
  271.4 0.1 select_bitcast_fusion
  271.5 9.8 %custom-call.9 = f32[2,1,64,64]{2,3,1,0:T(8,128)S(1)} custom-call(f32[2,1,64,64]{3,2,1,0:T(8,128)S(1)} %select_bitcast_fusion), custom_call_target="InvertDiagBlocksLowerTriangular" | custom-call | tf_op jit(solution)/shard_map/vmap(jit(_solve_triangular))/triangular_solve | solution.py:14
  281.3 1.3 fusion.4
  282.6 0.0 all-gather.5.cloned.1.call-update
  282.6 0.0 all-reduce.5.cloned.1.call-start
  282.7 18.8 %all-gather.5.cloned.1.call-done = f32[2,64,3072]{2,1,0:T(8,128)} async-done(((f32[2,64,768]{2,1,0:T(8,128)}), f32[2,64,3072]{2,1,0:T(8,128)}) %all-gather.5.cloned.1.call-update) | async-done | bytes 1572880 | tf_op jit(solution)/shard_map/all_gather | solution.py:37
  301.5 16.3 %convolution_convert_fusion.1 = bf16[2,64,768]{2,1,0:T(8,128)(2,1)} fusion(f32[2,64,3072]{2,1,0:T(8,128)} %all-gather.5.cloned.1.call-done, f32[2,3072,768]{2,1,0:T(8,128)} %convert_add_fusion), kind=kOutput, calls=%fused_computation.5 | convolution fusion | flops 3623976960 | bytes 20643840 | tf_op jit(solution)/shard_map/lrd,lde->lre/dot_general | solution.py:38
  317.8 70.8 %all-reduce.5.cloned.1.call-done = bf16[2,64,768]{2,1,0:T(8,128)(2,1)} async-done(((bf16[2,64,768]{2,1,0:T(8,128)(2,1)}), bf16[2,64,768]{2,1,0:T(8,128)(2,1)}) %all-reduce.5.cloned.1.call-update) | async-done | bytes 196624 | tf_op jit(solution)/shard_map/psum | solution.py:39
  388.6 20.9 %subtract_convert_fusion = bf16[2,3072,768]{2,1,0:T(8,128)(2,1)} fusion(f32[2,3072,768]{2,1,0:T(8,128)} %convert_add_fusion, f32[2,64,3072]{2,1,0:T(8,128)} %all-gather.5.cloned.1.call-done, bf16[2,64,768]{2,1,0:T(8,128)(2,1)} %all-reduce.5.cloned.1.call-done), kind=kOutput, calls=%fused_computation.1 | convolution fusion | flops 3633512448 | bytes 30081024 | tf_op jit(solution)/shard_map/lrd,lre->lde/dot_general | solution.py:46
  409.5 3.1 convolution_convert_fusion
  (19 shorter events, 0.2 us)
Async XLA Ops:
  7.2 91.5 %copy-start = (bf16[2,1024,768]{2,1,0:T(8,128)(2,1)S(1)}, bf16[2,1024,768]{2,1,0:T(8,128)(2,1)}, u32[]{:S(2)}) copy-start(bf16[2,1024,768]{2,1,0:T(8,128)(2,1)} %param.4) | copy-start | bytes 9437188
  7.2 91.5 %all-gather.3.cloned.1.call-start = ((), (), s32[]{:S(2)}) async-start(), calls=%async_computation.1 | async-start | bytes 15728640 | tf_op jit(solution)/shard_map/all_gather | solution.py:27
  12.0 105.9 %copy-start.4 = (f32[2,64,768]{2,1,0:T(8,128)S(1)}, f32[2,64,768]{2,1,0:T(8,128)}, u32[]{:S(2)}) copy-start(f32[2,64,768]{2,1,0:T(8,128)} %param.7) | copy-start | bytes 1179652
  12.0 156.6 %reduce-scatter.2.cloned.1.call-start = ((), (), s32[]{:S(2)}) async-start(), calls=%async_computation.2 | async-start | bytes 1966080 | tf_op jit(solution)/shard_map/reduce_scatter | solution.py:33
  140.5 103.4 %all-reduce.3.cloned.1.call-start = ((), (), s32[]{:S(2)}) async-start(), calls=%async_computation.3 | async-start | bytes 786432 | tf_op jit(solution)/shard_map/psum | solution.py:34
  168.7 132.8 %all-gather.5.cloned.1.call-start = ((), (), s32[]{:S(2)}) async-start(), calls=%async_computation.4 | async-start | bytes 1966080 | tf_op jit(solution)/shard_map/all_gather | solution.py:37
  243.9 37.5 %copy-start.2 = (f32[2,64,768]{2,1,0:T(8,128)S(1)}, f32[2,64,768]{2,1,0:T(8,128)}, u32[]{:S(2)}) copy-start(f32[2,64,768]{2,1,0:T(8,128)} %all-reduce.3.cloned.1.call-done) | copy-start | bytes 1179652
  282.6 106.0 %all-reduce.5.cloned.1.call-start = ((), (), s32[]{:S(2)}) async-start(), calls=%async_computation.5 | async-start | bytes 393216 | tf_op jit(solution)/shard_map/psum | solution.py:39
  388.6 20.9 %copy-start.3 = (bf16[2,64,768]{2,1,0:T(8,128)(2,1)S(1)}, bf16[2,64,768]{2,1,0:T(8,128)(2,1)}, u32[]{:S(2)}) copy-start(bf16[2,64,768]{2,1,0:T(8,128)(2,1)} %all-reduce.5.cloned.1.call-done) | copy-start | bytes 589828
  388.6 24.0 %copy-start.1 = (bf16[2,1024,768]{2,1,0:T(8,128)(2,1)S(1)}, bf16[2,1024,768]{2,1,0:T(8,128)(2,1)}, u32[]{:S(2)}) copy-start(bf16[2,1024,768]{2,1,0:T(8,128)(2,1)} %param.4) | copy-start | bytes 9437188
Sparse Core Ops, SparseCore 0:
  12.2 86.4 all-gather.2
  140.6 27.9 reduce-scatter.1
  172.0 71.8 all-reduce.2
  282.8 18.6 all-gather.4
  317.9 70.6 all-reduce.4
where the time goes:
time: 419 us
  waiting for transfers between devices  279 us (67%)
  matrix products  85 us (20%)
  other arithmetic  22 us (5%)
  between operations  13.9 us (3%)
  blocking collectives  10.9 us (3%)
  local copies, waits for them, and re-layouts  7.81 us (2%)
    all_gather x1, waiting for transfers between devices, compress(): lax.all_gather(out_grad, 'tensor', axis=1, tiled=True)  86.6 us
    psum x1, waiting for transfers between devices, compress(): left_part = lax.psum(left_part, 'dp')  75 us
    psum x1, waiting for transfers between devices, compress(): lax.psum(right_terms.astype(jnp.bfloat16), 'dp').astype(jnp.float32)  70.8 us
    reduce_scatter x1, waiting for transfers between devices, compress(): lax.psum_scatter(left_factor, 'tensor', scatter_dimension=2, tiled=True)  28.1 us
    dot_general x1, matrix products, compress(): jnp.einsum('lre,lde->lrd', right_init, moment, precision=lax.Precision.HI...  22.5 us
    dot_general x1, matrix products, compress(): jnp.einsum('lrd,lre->lde', ortho_basis, right_factor / replicas, precisio...  20.9 us
    dot_general x1, matrix products, compress(): jnp.einsum('ltd,lte->lde', lax.all_gather(out_grad, 'tensor', axis=1, til...  19.3 us
    all_gather x1, waiting for transfers between devices, compress(): ortho_basis = lax.all_gather(ortho_part, 'tensor', axis=2, tiled=True)  18.8 us
  transfers between devices with their start and end apart: 5, of which 5 were waited for; matrix products, arithmetic and copies ran while one was open for 0% of the time, Pallas kernels for 0%

commit v1 on v0

--- a/solution.py
+++ b/solution.py
@@ -31,7 +31,12 @@
     moment = moment + error_in.astype(jnp.float32)
     left_factor = jnp.einsum("lre,lde->lrd", right_init, moment, precision=lax.Precision.HIGHEST)
     left_part = lax.psum_scatter(left_factor, "tensor", scatter_dimension=2, tiled=True)
-    left_part = lax.psum(left_part, "dp")
+    peers = lax.axis_size("dp")
+    acc, far = (left_part, 1)
+    while far < peers:
+        acc = acc + lax.ppermute(acc, "dp", [(i, i ^ far) for i in range(peers)])
+        far = 2 * far
+    left_part = acc
     gram_matrix = lax.psum(gram_of(left_part), "tensor")
     ortho_part = solve_rows(gram_matrix, left_part)
     ortho_basis = lax.all_gather(ortho_part, "tensor", axis=2, tiled=True)

time: 419 us -> 385 us (0.919)
  waiting for transfers between devices: 279 us -> 239 us
  starting transfers between devices: 0.2 us -> 5.64 us
    psum x1 -> x0, waiting for transfers between devices: 75 us -> none  [compress(): left_part = lax.psum(left_part, 'dp')]
    ppermute x0 -> x3, waiting for transfers between devices: none -> 33.6 us  [compress(): acc = acc + lax.ppermute(acc, 'dp', [(i, i ^ far) for i in range(peers)])]
    ppermute x0 -> x3, starting transfers between devices: none -> 5.48 us  [compress(): acc = acc + lax.ppermute(acc, 'dp', [(i, i ^ far) for i in range(peers)])]
  transfers between devices with their start and end apart: 5 -> 7, of which waited for: 5 -> 7; matrix products, arithmetic and copies ran while one was open for 0% -> 0% of each run, Pallas kernels for 0% -> 0%
where the time goes in v1:
time: 385 us
  waiting for transfers between devices  239 us (62%)
  matrix products  83.8 us (22%)
  other arithmetic  23.2 us (6%)
  between operations  13.9 us (4%)
  blocking collectives  11.2 us (3%)
  local copies, waits for them, and re-layouts  7.76 us (2%)
  starting transfers between devices  5.64 us (1%)
    all_gather x1, waiting for transfers between devices, compress(): lax.all_gather(out_grad, 'tensor', axis=1, tiled=True)  86.6 us
    psum x1, waiting for transfers between devices, compress(): lax.psum(right_terms.astype(jnp.bfloat16), 'dp').astype(jnp.float32)  70.8 us
    ppermute x3, waiting for transfers between devices, compress(): acc = acc + lax.ppermute(acc, 'dp', [(i, i ^ far) for i in range(peers)])  33.6 us
    reduce_scatter x1, waiting for transfers between devices, compress(): lax.psum_scatter(left_factor, 'tensor', scatter_dimension=2, tiled=True)  28.1 us
    dot_general x1, matrix products, compress(): jnp.einsum('lre,lde->lrd', right_init, moment, precision=lax.Precision.HI...  22.5 us
    dot_general x1, matrix products, compress(): jnp.einsum('lrd,lre->lde', ortho_basis, right_factor / replicas, precisio...  20.9 us
    all_gather x1, waiting for transfers between devices, compress(): ortho_basis = lax.all_gather(ortho_part, 'tensor', axis=2, tiled=True)  20.2 us
    dot_general x1, matrix products, compress(): jnp.einsum('ltd,lte->lde', lax.all_gather(out_grad, 'tensor', axis=1, til...  19.2 us
  transfers between devices with their start and end apart: 7, of which 7 were waited for; matrix products, arithmetic and copies ran while one was open for 0% of the time, Pallas kernels for 0%

profile of v1, /device:TPU:0, one launch (start us, length us, event | category | flops | bytes accessed | tf_op | source)
XLA Modules:
  0.0 384.8 jit_solution(5790973538068934599)
XLA Ops:
  7.2 4.8 %copy.12 = bf16[2,256,3072]{1,2,0:T(8,128)(2,1)} copy(bf16[2,256,3072]{2,1,0:T(8,128)(2,1)} %param.5) | data formatting | bytes 6291456 | tf_op args[1]
  12.0 0.0 reduce-scatter.2.cloned.1.call-start
  12.1 86.6 %all-gather.3.cloned.1.call-done = bf16[2,1024,3072]{1,2,0:T(8,128)(2,1)} async-done(((bf16[2,256,3072]{1,2,0:T(8,128)(2,1)}), bf16[2,1024,3072]{1,2,0:T(8,128)(2,1)}) %all-gather.3.cloned.1.call-update) | async-done | bytes 12582928 | tf_op jit(solution)/shard_map/all_gather | solution.py:27
  98.7 19.2 %convert_add_fusion = f32[2,3072,768]{2,1,0:T(8,128)} fusion(bf16[2,3072,768]{2,1,0:T(8,128)(2,1)} %param.6, bf16[2,1024,3072]{1,2,0:T(8,128)(2,1)} %all-gather.3.cloned.1.call-done, bf16[2,1024,768]{2,1,0:T(8,128)(2,1)S(1)} %copy-done), kind=kOutput, calls=%fused_computation.2 | convolution fusion | flops 9673113600 | bytes 44040192 | tf_op jit(solution)/shard_map/ltd,lte->lde/dot_general | solution.py:25
  117.9 22.5 %convolution_bitcast_fusion = f32[2,64,3072]{2,1,0:T(8,128)} fusion(f32[2,3072,768]{2,1,0:T(8,128)} %convert_add_fusion, f32[2,64,768]{2,1,0:T(8,128)S(1)} %copy-done.3), kind=kOutput, calls=%fused_computation.3 | convolution fusion | flops 3623878656 | bytes 20840448 | tf_op jit(solution)/shard_map/lre,lde->lrd/dot_general | solution.py:32
  140.5 28.1 %reduce-scatter.2.cloned.1.call-done = f32[2,64,768]{2,1,0:T(8,128)} async-done(((f32[2,64,3072]{2,1,0:T(8,128)}), f32[2,64,768]{2,1,0:T(8,128)}) %reduce-scatter.2.cloned.1.call-update) | async-done | bytes 393232 | tf_op jit(solution)/shard_map/reduce_scatter | solution.py:33
  168.6 1.5 collective-permute-start
  170.1 9.4 %collective-permute-done = f32[2,64,768]{2,1,0:T(8,128)S(1)} collective-permute-done((f32[2,64,768]{2,1,0:T(8,128)}, f32[2,64,768]{2,1,0:T(8,128)S(1)}, u32[]{:S(2)}, u32[]{:S(2)}) %collective-permute-start) | collective-permute-done | bytes 393248 | tf_op jit(solution)/shard_map/ppermute | solution.py:37
  179.5 1.0 add.41
  180.6 1.5 collective-permute-start.1
  182.1 8.4 %collective-permute-done.1 = f32[2,64,768]{2,1,0:T(8,128)S(1)} collective-permute-done((f32[2,64,768]{2,1,0:T(8,128)S(1)}, f32[2,64,768]{2,1,0:T(8,128)S(1)}, u32[]{:S(2)}, u32[]{:S(2)}) %collective-permute-start.1) | collective-permute-done | bytes 393248 | tf_op jit(solution)/shard_map/ppermute | solution.py:37
  190.5 2.5 collective-permute-start.2
  193.0 0.1 copy.15
  193.1 15.8 %collective-permute-done.2 = f32[2,64,768]{2,1,0:T(8,128)S(1)} collective-permute-done((f32[2,64,768]{2,1,0:T(8,128)S(1)}, f32[2,64,768]{2,1,0:T(8,128)S(1)}, u32[]{:S(2)}, u32[]{:S(2)}) %collective-permute-start.2) | collective-permute-done | bytes 393248 | tf_op jit(solution)/shard_map/ppermute | solution.py:37
  208.9 0.1 add.43
  208.9 0.5 fusion.10
  209.4 11.2 %psum.14 = f32[2,64,64]{1,2,0:T(8,128)S(1)} all-reduce(f32[2,64,64]{1,2,0:T(8,128)S(1)} %fusion.10), channel_id=1, replica_groups=mesh['dp'=8,'tensor'=4] {'tensor'}, use_global_device_ids=true, to_apply=%region_1.0 | all-reduce | flops 8192 | bytes 65536 | tf_op jit(solution)/shard_map/psum | solution.py:40
  220.6 1.9 copy.14
  222.6 0.9 gather_fusion
  223.5 0.1 multiply_add_fusion
  223.6 0.1 copy.16
  223.6 0.1 fusion.6
  223.7 11.7 %custom-call.8 = f32[2,64,64]{2,1,0:T(8,128)S(1)} custom-call(f32[2,64,64]{2,1,0:T(8,128)S(1)} %fusion.6), custom_call_target="Cholesky" | custom-call | tf_op jit(solution)/shard_map/jit(cholesky)/cholesky | solution.py:11
  235.5 0.1 compare_reduce_fusion
  235.6 0.1 select_bitcast_fusion
  235.7 9.8 %custom-call.9 = f32[2,1,64,64]{2,3,1,0:T(8,128)S(1)} custom-call(f32[2,1,64,64]{3,2,1,0:T(8,128)S(1)} %select_bitcast_fusion), custom_call_target="InvertDiagBlocksLowerTriangular" | custom-call | tf_op jit(solution)/shard_map/vmap(jit(_solve_triangular))/triangular_solve | solution.py:14
  245.5 1.3 fusion.4
  246.9 20.2 %all-gather.5.cloned.1.call-done = f32[2,64,3072]{2,1,0:T(8,128)} async-done(((f32[2,64,768]{2,1,0:T(8,128)}), f32[2,64,3072]{2,1,0:T(8,128)}) %all-gather.5.cloned.1.call-update) | async-done | bytes 1572880 | tf_op jit(solution)/shard_map/all_gather | solution.py:42
  267.1 16.3 %convolution_convert_fusion.1 = bf16[2,64,768]{2,1,0:T(8,128)(2,1)} fusion(f32[2,64,3072]{2,1,0:T(8,128)} %all-gather.5.cloned.1.call-done, f32[2,3072,768]{2,1,0:T(8,128)} %convert_add_fusion), kind=kOutput, calls=%fused_computation.5 | convolution fusion | flops 3623976960 | bytes 20643840 | tf_op jit(solution)/shard_map/lrd,lde->lre/dot_general | solution.py:43
  283.5 70.8 %all-reduce.2.cloned.1.call-done = bf16[2,64,768]{2,1,0:T(8,128)(2,1)} async-done(((bf16[2,64,768]{2,1,0:T(8,128)(2,1)}), bf16[2,64,768]{2,1,0:T(8,128)(2,1)}) %all-reduce.2.cloned.1.call-update) | async-done | bytes 196624 | tf_op jit(solution)/shard_map/psum | solution.py:44
  354.3 20.9 %subtract_convert_fusion = bf16[2,3072,768]{2,1,0:T(8,128)(2,1)} fusion(f32[2,3072,768]{2,1,0:T(8,128)} %convert_add_fusion, f32[2,64,3072]{2,1,0:T(8,128)} %all-gather.5.cloned.1.call-done, bf16[2,64,768]{2,1,0:T(8,128)(2,1)} %all-reduce.2.cloned.1.call-done), kind=kOutput, calls=%fused_computation.1 | convolution fusion | flops 3633512448 | bytes 30081024 | tf_op jit(solution)/shard_map/lrd,lre->lde/dot_general | solution.py:51
  375.2 3.1 convolution_convert_fusion
  (23 shorter events, 0.4 us)
Async XLA Ops:
  7.2 91.5 %copy-start = (bf16[2,1024,768]{2,1,0:T(8,128)(2,1)S(1)}, bf16[2,1024,768]{2,1,0:T(8,128)(2,1)}, u32[]{:S(2)}) copy-start(bf16[2,1024,768]{2,1,0:T(8,128)(2,1)} %param.4) | copy-start | bytes 9437188
  7.2 91.5 %all-gather.3.cloned.1.call-start = ((), (), s32[]{:S(2)}) async-start(), calls=%async_computation.1 | async-start | bytes 15728640 | tf_op jit(solution)/shard_map/all_gather | solution.py:27
  12.0 105.9 %copy-start.3 = (f32[2,64,768]{2,1,0:T(8,128)S(1)}, f32[2,64,768]{2,1,0:T(8,128)}, u32[]{:S(2)}) copy-start(f32[2,64,768]{2,1,0:T(8,128)} %param.7) | copy-start | bytes 1179652
  12.0 156.6 %reduce-scatter.2.cloned.1.call-start = ((), (), s32[]{:S(2)}) async-start(), calls=%async_computation.2 | async-start | bytes 1966080 | tf_op jit(solution)/shard_map/reduce_scatter | solution.py:33
  140.5 126.7 %all-gather.5.cloned.1.call-start = ((), (), s32[]{:S(2)}) async-start(), calls=%async_computation.3 | async-start | bytes 1966080 | tf_op jit(solution)/shard_map/all_gather | solution.py:42
  168.6 10.9 %collective-permute-start = (f32[2,64,768]{2,1,0:T(8,128)}, f32[2,64,768]{2,1,0:T(8,128)S(1)}, u32[]{:S(2)}, u32[]{:S(2)}) collective-permute-start(f32[2,64,768]{2,1,0:T(8,128)} %reduce-scatter.2.cloned.1.call-done), channel_id=1, source_target_pairs={{0,4},{4,0},{8,12},{12,8},{16,20},{20,16},{24,28},{28,24},{1,5},{5... | collective-permute-start | bytes 1179656 | tf_op jit(solution)/shard_map/ppermute | solution.py:37
  180.6 9.9 %collective-permute-start.1 = (f32[2,64,768]{2,1,0:T(8,128)S(1)}, f32[2,64,768]{2,1,0:T(8,128)S(1)}, u32[]{:S(2)}, u32[]{:S(2)}) collective-permute-start(f32[2,64,768]{2,1,0:T(8,128)S(1)} %add.41), channel_id=1, source_target_pairs={{0,8},{4,12},{8,0},{12,4},{16,24},{20,28},{24,16},{28,20},{1,9},{5... | collective-permute-start | bytes 1179656 | tf_op jit(solution)/shard_map/ppermute | solution.py:37
  190.5 18.4 %collective-permute-start.2 = (f32[2,64,768]{2,1,0:T(8,128)S(1)}, f32[2,64,768]{2,1,0:T(8,128)S(1)}, u32[]{:S(2)}, u32[]{:S(2)}) collective-permute-start(f32[2,64,768]{2,1,0:T(8,128)S(1)} %add.42), channel_id=1, source_target_pairs={{0,16},{4,20},{8,24},{12,28},{16,0},{20,4},{24,8},{28,12},{1,17},{... | collective-permute-start | bytes 1179656 | tf_op jit(solution)/shard_map/ppermute | solution.py:37
  246.8 107.5 %all-reduce.2.cloned.1.call-start = ((), (), s32[]{:S(2)}) async-start(), calls=%async_computation.4 | async-start | bytes 393216 | tf_op jit(solution)/shard_map/psum | solution.py:44
  354.3 20.9 %copy-start.2 = (bf16[2,64,768]{2,1,0:T(8,128)(2,1)S(1)}, bf16[2,64,768]{2,1,0:T(8,128)(2,1)}, u32[]{:S(2)}) copy-start(bf16[2,64,768]{2,1,0:T(8,128)(2,1)} %all-reduce.2.cloned.1.call-done) | copy-start | bytes 589828
  354.3 24.0 %copy-start.1 = (bf16[2,1024,768]{2,1,0:T(8,128)(2,1)S(1)}, bf16[2,1024,768]{2,1,0:T(8,128)(2,1)}, u32[]{:S(2)}) copy-start(bf16[2,1024,768]{2,1,0:T(8,128)(2,1)} %param.4) | copy-start | bytes 9437188
Sparse Core Ops, SparseCore 0:
  12.2 86.4 all-gather.2
  140.6 27.9 reduce-scatter.1
  247.0 20.1 all-gather.4
  283.6 70.6 all-reduce.1
